TPU v7x, 32 devices: a whole 2x2x4 slice. The times are simulated.
32 devices in a mesh: dp: 4 (over z), ctx: 8 (over y, x, core).
Axes of the slice: x: 2, y: 2, z: 4, core: 2. Of those that a mesh axis runs over, the one named last changes fastest.
Arguments:
- inputs: bfloat16 [4, 1024, 1024], P('dp', 'ctx'), may hold values from -6 to 6
- cotangent: bfloat16 [4, 1024, 1024], P('dp', 'ctx'), may hold values from -6 to 6
- mixer_params: float32 [4194304], P(('dp', 'ctx')), may hold values from -0.1875 to 0.1875
- mixer_first: float32 [4194304], P(('dp', 'ctx')), may hold values from -0.0014648438 to 0.0014648438
- mixer_second: float32 [4194304], P(('dp', 'ctx')), may hold values from 2.3434208e-11 to 2.3434207e-10
- ffn_params: float32 [4325376], P(('dp', 'ctx')), may hold values from -0.21320072 to 0.21320072
- ffn_first: float32 [4325376], P(('dp', 'ctx')), may hold values from -0.0014648438 to 0.0014648438
- ffn_second: float32 [4325376], P(('dp', 'ctx')), may hold values from 2.3434208e-11 to 2.3434207e-10
- small_params: float32 [14852], replicated, may hold values from -7 to 2.8
- small_first: float32 [14852], replicated, may hold values from -0.0014648438 to 0.0014648438
- small_second: float32 [14852], replicated, may hold values from 2.3434208e-11 to 2.3434208e-07
Outputs:
- outputs: bfloat16 [4, 1024, 1024], P('dp', 'ctx')
- grad_inputs: bfloat16 [4, 1024, 1024], P('dp', 'ctx')
- mixer_grad: float32 [4194304], P(('dp', 'ctx'))
- ffn_grad: float32 [4325376], P(('dp', 'ctx'))
- small_grad: float32 [14852], replicated
- mixer_new: float32 [4194304], P(('dp', 'ctx'))
- mixer_first_new: float32 [4194304], P(('dp', 'ctx'))
- mixer_second_new: float32 [4194304], P(('dp', 'ctx'))
- ffn_new: float32 [4325376], P(('dp', 'ctx'))
- ffn_first_new: float32 [4325376], P(('dp', 'ctx'))
- ffn_second_new: float32 [4325376], P(('dp', 'ctx'))
- small_new: float32 [14852], replicated
- small_first_new: float32 [14852], replicated
- small_second_new: float32 [14852], replicated
All inputs are finite; a program needn't handle non-finite values.
Results may differ from a plain program's by a relative error of at most 0.013.
Values may be sent and summed in bfloat16 or wider, within the bound.
A program may use at most 320 MiB of HBM per device.

v0:
```python
import jax
import jax.numpy as jnp
from jax import lax
from jax.sharding import PartitionSpec as P

D = 1024
H = 2
DK = 256
DV = 512
FF = 1408
CONV = 4
GROUP = 64


EPSILON = 1e-06
ADAM_EPS = 1e-08
LEARN_RATE = 0.02
BETA_ONE = 0.9
BETA_TWO = 0.999
DECAY_RATE = 0.1
CORRECT_ONE = 1.0 - 0.9**3
CORRECT_TWO = 1.0 - 0.999**3
MAX_NORM = 1.0
HIGHEST = lax.Precision.HIGHEST


def from_behind(value, axis, steps):
    count = lax.axis_size(axis)
    initial, last = (max(0, -steps), min(count, count - steps))
    return lax.ppermute(value, axis, [(source, source + steps) for source in range(initial, last)])


def entering(array, axis, combine, identity):
    devices, position = (lax.axis_size(axis), lax.axis_index(axis))
    everything = jax.tree.map(
        lambda part, kind: lax.all_gather(part.astype(kind), axis),
        array,
        (jnp.bfloat16, jnp.bfloat16),
    )
    start = jax.tree.map(
        lambda part, zero: jnp.broadcast_to(jnp.asarray(zero, part.dtype), part.shape),
        array,
        identity,
    )

    def lap(k, before):
        reached = k < position
        new = combine(
            before, jax.tree.map(lambda part, own: part[k].astype(own.dtype), everything, array)
        )
        return jax.tree.map(lambda a, b: jnp.where(reached, a, b), new, before)

    return lax.fori_loop(0, devices, lap, start)


def carried_in(array, axis, join, neutral):
    count = lax.axis_size(axis)
    place = lax.axis_index(axis)
    ahead = count - 1 - place
    gathered = jax.tree.map(
        lambda a, kind: lax.all_gather(a.astype(kind), axis),
        array,
        jax.tree.map(lambda a: jnp.bfloat16 if a.dtype == jnp.float32 else a.dtype, array),
    )
    state = jax.tree.map(lambda a, e: jnp.zeros_like(a) + jnp.asarray(e, a.dtype), array, neutral)

    def one(lap, state):
        source = count - 1 - lap
        return join(
            state,
            jax.tree.map(
                lambda a, own: lax.dynamic_index_in_dim(a, source, 0, False).astype(own.dtype),
                gathered,
                array,
            ),
        )

    return lax.fori_loop(0, ahead, one, state)


def norm_scale(values, gain):
    return values * lax.rsqrt(jnp.mean(values * values, axis=-1, keepdims=True) + EPSILON) * gain


def swiglu(gate_part, up_part):
    return jax.nn.silu(gate_part) * up_part


def unpack_small(packed):
    width = 2 * H * DK + H * DV
    lengths = [D, D, DV, CONV * width, D * 2 * H, H, H]
    pieces = []
    offset = 0
    for length in lengths:
        pieces.append(packed[offset : offset + length])
        offset = offset + length
    return (
        pieces[0],
        pieces[1],
        pieces[2],
        pieces[3].reshape(CONV, width),
        pieces[4].reshape(D, 2 * H),
        pieces[5],
        pieces[6],
    )


def split_weights(mix_whole, ffn_whole):
    mix_rows = mix_whole.reshape(-1, D)
    ffn_rows = ffn_whole.reshape(-1, D)
    edge = 2 * H * DK + 2 * H * DV
    return (mix_rows[:edge], mix_rows[edge:], ffn_rows[: 2 * FF], ffn_rows[2 * FF :])


def features(extended, tap_values, gate_logits, a_log, dt_bias):
    count = extended.shape[0] - (CONV - 1)
    summed = tap_values[0] * extended[0:count]
    for tap_index in range(1, CONV):
        summed = summed + tap_values[tap_index] * extended[tap_index : tap_index + count]
    activated = jax.nn.silu(summed)
    query_part = activated[:, : H * DK].reshape(count, H, DK)
    key_part = activated[:, H * DK : 2 * H * DK].reshape(count, H, DK)
    value_part = activated[:, 2 * H * DK :].reshape(count, H, DV)
    query = (
        query_part
        * lax.rsqrt(jnp.sum(query_part * query_part, axis=-1, keepdims=True) + EPSILON)
        * DK ** (-0.5)
    )
    keys = key_part * lax.rsqrt(jnp.sum(key_part * key_part, axis=-1, keepdims=True) + EPSILON)
    beta = jax.nn.sigmoid(gate_logits[:, :H])
    decay = -jnp.exp(a_log) * jax.nn.softplus(gate_logits[:, H:] + dt_bias)
    return (
        jnp.transpose(query, (1, 0, 2)),
        jnp.transpose(keys, (1, 0, 2)),
        jnp.transpose(value_part, (1, 0, 2)),
        beta.T,
        decay.T,
    )


def split_groups(values):
    blocks = values.shape[1] // GROUP
    shaped = values.reshape((values.shape[0], blocks, GROUP) + values.shape[2:])
    return jnp.moveaxis(shaped, 1, 0)


def group_parts(key_block, value_block, beta_block, decay_block):
    size = decay_block.shape[-1]
    cumulative = jnp.cumsum(decay_block, axis=-1)
    row_index = lax.broadcasted_iota(jnp.int32, (size, size), 0)
    col_index = lax.broadcasted_iota(jnp.int32, (size, size), 1)
    lower = row_index >= col_index
    strict = row_index > col_index
    spread = jnp.where(lower, cumulative[:, :, None] - cumulative[:, None, :], 0.0)
    decay_matrix = jnp.where(lower, jnp.exp(spread), 0.0)
    key_gram = jnp.einsum("hid,hjd->hij", key_block, key_block, precision=HIGHEST)
    system = jnp.where(strict, beta_block[:, :, None] * key_gram * decay_matrix, 0.0) + jnp.eye(
        size, dtype=key_block.dtype
    )
    right_side = jnp.concatenate(
        [
            key_block * (beta_block * jnp.exp(cumulative))[:, :, None],
            value_block * beta_block[:, :, None],
        ],
        axis=-1,
    )
    solved = jax.scipy.linalg.solve_triangular(system, right_side, lower=True, unit_diagonal=True)
    key_mix = solved[..., :DK]
    value_mix = solved[..., DK:]
    last_decay = cumulative[:, -1]
    keys_to_end = key_block * jnp.exp(last_decay[:, None] - cumulative)[:, :, None]
    return (cumulative, decay_matrix, key_mix, value_mix, last_decay, keys_to_end)


def group_run(state, pieces):
    query_block, key_block, value_block, beta_block, decay_block = pieces
    cumulative, decay_matrix, key_mix, value_mix, last_decay, keys_to_end = group_parts(
        key_block, value_block, beta_block, decay_block
    )
    pseudo_values = value_mix - jnp.einsum("hcd,hde->hce", key_mix, state, precision=HIGHEST)
    scores = jnp.einsum("hid,hjd->hij", query_block, key_block, precision=HIGHEST) * decay_matrix
    block_out = jnp.einsum(
        "hcd,hde->hce", query_block * jnp.exp(cumulative)[:, :, None], state, precision=HIGHEST
    )
    block_out = block_out + jnp.einsum("hij,hje->hie", scores, pseudo_values, precision=HIGHEST)
    next_state = jnp.exp(last_decay)[:, None, None] * state + jnp.einsum(
        "hcd,hce->hde", keys_to_end, pseudo_values, precision=HIGHEST
    )
    return (next_state, block_out)


def mixer_run(state, query, keys, values, beta, decay):
    pieces = (
        split_groups(query),
        split_groups(keys),
        split_groups(values),
        split_groups(beta),
        split_groups(decay),
    )
    final_state, blocks_out = lax.scan(group_run, state, pieces)
    joined = jnp.moveaxis(blocks_out, 0, 1)
    return (joined.reshape(joined.shape[0], -1, joined.shape[-1]), final_state)


def combine(earlier, later):
    first_map, first_shift = earlier
    second_map, second_shift = later
    composed = jnp.einsum("hij,hjk->hik", second_map, first_map, precision=HIGHEST)
    shifted = jnp.einsum("hij,hjk->hik", second_map, first_shift, precision=HIGHEST) + second_shift
    return (composed, shifted)


def transition(keys, values, beta, decay):
    pieces = (split_groups(keys), split_groups(values), split_groups(beta), split_groups(decay))
    start = (
        jnp.broadcast_to(jnp.eye(DK, dtype=jnp.float32), (H, DK, DK)),
        jnp.zeros((H, DK, DV), jnp.float32),
    )

    def step_block(carry, piece):
        key_block, value_block, beta_block, decay_block = piece
        cumulative, decay_matrix, key_mix, value_mix, last_decay, keys_to_end = group_parts(
            key_block, value_block, beta_block, decay_block
        )
        block_map = jnp.exp(last_decay)[:, None, None] * jnp.eye(
            DK, dtype=key_block.dtype
        ) - jnp.einsum("hcd,hce->hde", keys_to_end, key_mix, precision=HIGHEST)
        block_shift = jnp.einsum("hcd,hce->hde", keys_to_end, value_mix, precision=HIGHEST)
        return (combine(carry, (block_map, block_shift)), None)

    result, unused = lax.scan(step_block, start, pieces)
    return result


def gated_norm(mixed, out_gate, gain_head):
    count = out_gate.shape[0]
    heads = jnp.transpose(mixed, (1, 0, 2))
    normed = norm_scale(heads, gain_head)
    return (normed * jax.nn.silu(out_gate.reshape(count, H, DV))).reshape(count, H * DV)


def adam_step(weight, grad_full, first, second, clip):
    grad_clipped = grad_full * clip
    first_new = BETA_ONE * first + (1.0 - BETA_ONE) * grad_clipped
    second_new = BETA_TWO * second + (1.0 - BETA_TWO) * grad_clipped * grad_clipped
    update = (
        first_new / CORRECT_ONE / (jnp.sqrt(second_new / CORRECT_TWO) + ADAM_EPS)
        + DECAY_RATE * weight
    )
    return (weight - LEARN_RATE * update, first_new, second_new)


def body(
    inputs,
    cotangent,
    mixer_params,
    mixer_first,
    mixer_second,
    ffn_params,
    ffn_first,
    ffn_second,
    small_params,
    small_first,
    small_second,
):
    gain_one, gain_two, gain_head, tap_values, w_gates, a_log, dt_bias = unpack_small(small_params)
    width = tap_values.shape[1]
    mix_part = mixer_params.astype(jnp.bfloat16)
    ffn_part = ffn_params.astype(jnp.bfloat16)
    mix_whole, ffn_whole = (
        lax.all_gather(mix_part, ("dp", "ctx"), axis=0, tiled=True),
        lax.all_gather(ffn_part, ("dp", "ctx"), axis=0, tiled=True),
    )
    w_in, w_out, w_ffn, w_down = split_weights(mix_whole, ffn_whole)
    x_float = inputs[0].astype(jnp.float32)
    count = x_float.shape[0]
    normed_in = norm_scale(x_float, gain_one).astype(jnp.bfloat16)
    projected = jnp.dot(normed_in, w_in.T, preferred_element_type=jnp.float32)
    gate_logits = jnp.dot(normed_in.astype(jnp.float32), w_gates, precision=HIGHEST)
    conv_pre = projected[:, :width]
    out_gate = projected[:, width:]
    border = from_behind(conv_pre[count - (CONV - 1) :], "ctx", 1)
    extended = jnp.concatenate([border, conv_pre], axis=0)
    query, keys, values, beta, decay = features(extended, tap_values, gate_logits, a_log, dt_bias)
    maps = transition(keys, values, beta, decay)
    eye_stack = jnp.broadcast_to(jnp.eye(DK, dtype=jnp.float32), (H, DK, DK))
    zero_stack = jnp.zeros((H, DK, DV), jnp.float32)
    prefix = entering((maps[0], maps[1]), "ctx", combine, (eye_stack, zero_stack))
    state_in = prefix[1]
    mixed, final_state = mixer_run(state_in, query, keys, values, beta, decay)
    head_out = gated_norm(mixed, out_gate, gain_head).astype(jnp.bfloat16)
    resid = x_float + jnp.dot(head_out, w_out, preferred_element_type=jnp.float32)
    normed_mid = norm_scale(resid, gain_two).astype(jnp.bfloat16)
    ffn_pre = jnp.dot(normed_mid, w_ffn.T, preferred_element_type=jnp.float32)
    gate_part = ffn_pre[:, :FF]
    up_part = ffn_pre[:, FF:]
    hidden_act = swiglu(gate_part, up_part).astype(jnp.bfloat16)
    result = (resid + jnp.dot(hidden_act, w_down, preferred_element_type=jnp.float32)).astype(
        jnp.bfloat16
    )
    seq_grad = cotangent[0]
    grad_float = seq_grad.astype(jnp.float32)
    grad_down = jnp.dot(hidden_act.T, seq_grad, preferred_element_type=jnp.float32)
    grad_hidden = jnp.dot(seq_grad, w_down.T, preferred_element_type=jnp.float32)
    unused_one, pull_swiglu = jax.vjp(swiglu, gate_part, up_part)
    grad_gate, grad_up = pull_swiglu(grad_hidden)
    grad_pre = jnp.concatenate([grad_gate, grad_up], axis=1).astype(jnp.bfloat16)
    grad_ffn = jnp.dot(grad_pre.T, normed_mid, preferred_element_type=jnp.float32)
    grad_mid = jnp.dot(grad_pre, w_ffn, preferred_element_type=jnp.float32)
    unused_two, pull_mid = jax.vjp(norm_scale, resid, gain_two)
    grad_through, grad_gain_two = pull_mid(grad_mid)
    grad_resid = grad_float + grad_through
    ffn_flat = jnp.concatenate([grad_ffn, grad_down], axis=0).reshape(-1)
    ffn_shard = lax.psum_scatter(ffn_flat, ("dp", "ctx"), scatter_dimension=0, tiled=True)
    resid_half = grad_resid.astype(jnp.bfloat16)
    grad_out = jnp.dot(head_out.T, resid_half, preferred_element_type=jnp.float32)
    grad_head = jnp.dot(resid_half, w_out.T, preferred_element_type=jnp.float32)
    unused_three, pull_gated = jax.vjp(gated_norm, mixed, out_gate, gain_head)
    grad_mixed, grad_gate_out, grad_gain_head = pull_gated(grad_head)
    unused_four, pull_mixer = jax.vjp(mixer_run, state_in, query, keys, values, beta, decay)
    local_term = pull_mixer((grad_mixed, jnp.zeros_like(final_state)))[0]
    flipped = jnp.transpose(maps[0], (0, 2, 1))
    suffix = carried_in((flipped, local_term), "ctx", combine, (eye_stack, zero_stack))
    mixer_grads = pull_mixer((grad_mixed, suffix[1]))
    unused_five, pull_feat = jax.vjp(features, extended, tap_values, gate_logits, a_log, dt_bias)
    grad_ext, grad_taps, grad_logits, grad_alog, grad_bias = pull_feat(mixer_grads[1:])
    returned = from_behind(grad_ext[: CONV - 1], "ctx", -1)
    grad_conv = grad_ext[CONV - 1 :].at[count - (CONV - 1) :].add(returned)
    grad_proj = jnp.concatenate([grad_conv, grad_gate_out], axis=1).astype(jnp.bfloat16)
    grad_in = jnp.dot(grad_proj.T, normed_in, preferred_element_type=jnp.float32)
    grad_normed = jnp.dot(grad_proj, w_in, preferred_element_type=jnp.float32) + jnp.dot(
        grad_logits, w_gates.T, precision=HIGHEST
    )
    grad_gates = jnp.dot(normed_in.astype(jnp.float32).T, grad_logits, precision=HIGHEST)
    unused_six, pull_in = jax.vjp(norm_scale, x_float, gain_one)
    grad_x, grad_gain_one = pull_in(grad_normed)
    grad_input = (grad_resid + grad_x).astype(jnp.bfloat16)
    mix_flat = jnp.concatenate([grad_in, grad_out], axis=0).reshape(-1)
    mix_shard = lax.psum_scatter(mix_flat, ("dp", "ctx"), scatter_dimension=0, tiled=True)
    small_local = jnp.concatenate(
        [
            grad_gain_one,
            grad_gain_two,
            grad_gain_head,
            grad_taps.reshape(-1),
            grad_gates.reshape(-1),
            grad_alog,
            grad_bias,
        ]
    )
    shard_squares = jnp.sum(mix_shard * mix_shard) + jnp.sum(ffn_shard * ffn_shard)
    small_grad, total_squares = lax.psum((small_local, shard_squares), ("dp", "ctx"))
    squares = total_squares + jnp.sum(small_grad * small_grad)
    clip = jnp.minimum(1.0, MAX_NORM / (jnp.sqrt(squares) + 1e-06))
    mixer_new, mixer_first_new, mixer_second_new = adam_step(
        mixer_params, mix_shard, mixer_first, mixer_second, clip
    )
    ffn_new, ffn_first_new, ffn_second_new = adam_step(
        ffn_params, ffn_shard, ffn_first, ffn_second, clip
    )
    small_new, small_first_new, small_second_new = adam_step(
        small_params, small_grad, small_first, small_second, clip
    )
    return (
        result[None],
        grad_input[None],
        mix_shard,
        ffn_shard,
        small_grad,
        mixer_new,
        mixer_first_new,
        mixer_second_new,
        ffn_new,
        ffn_first_new,
        ffn_second_new,
        small_new,
        small_first_new,
        small_second_new,
    )


def solution(mesh):
    return jax.shard_map(
        body,
        mesh=mesh,
        in_specs=(
            P("dp", "ctx", None),
            P("dp", "ctx", None),
            P(("dp", "ctx")),
            P(("dp", "ctx")),
            P(("dp", "ctx")),
            P(("dp", "ctx")),
            P(("dp", "ctx")),
            P(("dp", "ctx")),
            P(),
            P(),
            P(),
        ),
        out_specs=(
            P("dp", "ctx", None),
            P("dp", "ctx", None),
            P(("dp", "ctx")),
            P(("dp", "ctx")),
            P(),
            P(("dp", "ctx")),
            P(("dp", "ctx")),
            P(("dp", "ctx")),
            P(("dp", "ctx")),
            P(("dp", "ctx")),
            P(("dp", "ctx")),
            P(),
            P(),
            P(),
        ),
        check_vma=False,
    )
```

profile of v0, /device:TPU:0, one launch (start us, length us, event | category | flops | bytes accessed | tf_op | source)
XLA Modules:
  0.0 1128.1 jit_solution(17236866343093623935)
XLA Ops:
  13.7 77.5 %all-gather.11.cloned.1.call-done = bf16[4194304]{0:T(1024)(128)(2,1)} async-done(((bf16[131072]{0:T(1024)(128)(2,1)}), bf16[4194304]{0:T(1024)(128)(2,1)}) %all-gather.11.cloned.1.call-update) | async-done | bytes 8388624 | tf_op jit(solution)/shard_map/all_gather | solution.py:271
  91.2 6.4 slice.294
  97.7 10.3 slice.251
  108.0 5.0 fusion.320
  113.0 2.2 collective-permute-start
  121.7 38.8 %while.160 = (s32[]{:T(128)}, f32[2,256,256]{2,1,0:T(8,128)}, f32[2,256,512]{2,1,0:T(8,128)}, f32[2,2,64]{2,1,0:T(2,128)}, f32[2,2,64,256]{3,2,1,0:T(8,128)S(1)}...) while((s32[]{:T(128)}, f32[2,256,256]{2,1,0:T(8,128)}, ...), condition=%wide.region_4.6_spmd.clone, body=%wide.region_2.5_spmd.clone.sunk | while | flops 1611903232 | bytes 17252060 | solution.py:231
  124.1 9.8 custom-call.53
  143.5 9.8 custom-call.53
  167.9 3.2 slice.305
  171.1 4.2 slice.267
  175.4 4.2 slice.275
  183.7 6.1 slice.306
  189.8 9.7 slice.270
  199.5 3.0 slice.309
  202.5 5.5 slice.274
  208.1 31.5 %all-gather.17.cloned.1.call-done = bf16[16,256,512]{2,1,0:T(8,128)(2,1)} async-done(((bf16[2,256,512]{2,1,0:T(8,128)(2,1)}), bf16[16,256,512]{2,1,0:T(8,128)(2,1)}) %all-gather.17.cloned.1.call-update) | async-done | bytes 4194320 | tf_op jit(solution)/shard_map/all_gather | solution.py:36
  239.6 16.6 %while.161 = (s32[]{:T(128)}, f32[2,256,512]{2,1,0:T(8,128)S(1)}, s32[]{:T(128)}, bf16[8,2,256,256]{3,2,1,0:T(8,128)(2,1)}, bf16[8,2,256,512]{3,2,1,0:T(8,128)(2,1)}, /*index=5*/s32[]{:T(128)}, s32[]{:T(128)}) while((s32[]{:T(128)}, f32[2,256,512]{2,1,0:T(8,128)S(1)}, s32[]{:T(128)}, bf16[8,2,256,256]{3,2,1,0:T(8,128)(2,1)}, ...), condition=%wide.region_6.8_spmd.clone, body=%wide.region_5.7_spmd.clone.sunk | while | flops 806617088 | bytes 6031975 | solution.py:53
  257.2 52.2 %while.156 = (s32[]{:T(128)}, f32[2,256,512]{2,1,0:T(8,128)S(1)}, f32[2,2,64,512]{3,2,1,0:T(8,128)}, f32[2,2,64]{2,1,0:T(2,128)}, f32[2,2,64,256]{3,2,1,0:T(8,12...) while((s32[]{:T(128)}, f32[2,256,512]{2,1,0:T(8,128)S(1)}, ...), condition=%wide.region_10.12_spmd, body=%wide.region_8.11_spmd.sunk | while | flops 781201600 | bytes 15008757 | solution.py:200
  260.1 2.4 fusion.477
  266.8 11.2 custom-call.50
  286.3 2.4 fusion.477
  292.9 11.2 custom-call.50
  315.2 3.0 multiply_reduce_fusion.9
  321.2 69.0 %while.158 = (s32[]{:T(128)}, f32[2,256,512]{2,1,0:T(8,128)S(1)}, f32[2,2,64,64]{3,2,1,0:T(8,128)}, f32[2,2,64,64]{3,2,1,0:T(8,128)}, f32[2,2,64,1]{2,1,3,0:T(2,...) while((s32[]{:T(128)}, f32[2,256,512]{2,1,0:T(8,128)S(1)}, ...), condition=%wide.region_17.19_spmd.clone.clone, body=%wide.region_15.18_spmd.clone.clone.sunk | while | flops 529560128 | bytes 10886193 | solution.py:200
  330.0 11.2 custom-call.51
  341.2 2.2 bitcast_dynamic-update-slice_fusion.18
  359.6 11.2 custom-call.51
  370.8 2.2 bitcast_dynamic-update-slice_fusion.18
  390.2 5.0 fusion.317
  402.4 15.0 %while.162 = (s32[]{:T(128)}, f32[2,256,512]{2,1,0:T(8,128)S(1)}, f32[2,2,1,1]{1,3,2,0:T(1,128)}, f32[2,2,64,256]{3,2,1,0:T(8,128)}, f32[2,2,64,512]{3,2,1,0:T(8...) while((s32[]{:T(128)}, f32[2,256,512]{2,1,0:T(8,128)S(1)}, ...), condition=%wide.region_19.21_spmd.clone, body=%wide.region_18.20_spmd.clone.sunk | while | flops 655753216 | bytes 7277727 | solution.py:200
  420.2 3.4 fusion.289
  425.4 5.7 maximum_bitcast_fusion
  431.1 8.3 copy.331
  439.4 2.7 fusion.296
  442.2 12.9 %all-gather.21.cloned.1.call-done = bf16[16,256,512]{2,1,0:T(8,128)(2,1)} async-done(((bf16[2,256,512]{2,1,0:T(8,128)(2,1)}), bf16[16,256,512]{2,1,0:T(8,128)(2,1)}) %all-gather.21.cloned.1.call-update) | async-done | bytes 4194320 | tf_op jit(solution)/shard_map/all_gather | solution.py:61
  455.3 13.4 %while.157 = (s32[]{:T(128)}, f32[2,256,512]{2,1,0:T(8,128)S(1)}, s32[]{:T(128)}, bf16[8,2,256,256]{3,2,1,0:T(8,128)(2,1)}, bf16[8,2,256,512]{3,2,1,0:T(8,128)(2...) while((s32[]{:T(128)}, f32[2,256,512]{2,1,0:T(8,128)S(1)}, s32[]{:T(128)}, ...), condition=%wide.region_21.23_spmd, body=%wide.region_20.22_spmd.sunk | while | flops 805830656 | bytes 4981907 | solution.py:78
  472.2 67.0 %while.159 = (s32[]{:T(128)}, f32[2,256,512]{2,1,0:T(8,128)S(1)}, f32[2,2,64,256]{3,2,0,1:T(8,128)}, f32[2,2,64,256]{3,2,0,1:T(8,128)}, f32[2,2,64,512]{3,2,0,1:...) while((s32[]{:T(128)}, f32[2,256,512]{2,1,0:T(8,128)S(1)}, ...), condition=%wide.region_33.35_spmd.clone.clone, body=%wide.region_22.34_spmd.clone.clone.sunk | while | flops 1569133696 | bytes 51536812 | solution.py:200
  479.0 9.8 custom-call.52
  489.3 2.1 fusion.517
  512.3 9.8 custom-call.52
  522.7 2.1 fusion.517
  551.6 5.3 maximum_bitcast_fusion.1
  556.9 8.1 copy.330
  566.2 3.1 fusion.238
  570.7 3.9 fusion.274
  576.6 491.6 %all-reduce.22.cloned.1.call-done = (f32[4194304]{0:T(1024)}, f32[4325376]{0:T(1024)}) async-done(((f32[4194304]{0:T(1024)}, f32[4325376]{0:T(1024)}), (f32[4194304]{0:T(1024)}, f32[4325376]{0:T(1024)})) %all-reduce.22.cloned.1.call-update) | async-done | bytes 34078736
  1073.2 40.8 %all-reduce.18 = (f32[14852]{0:T(1024)S(1)}, f32[]{:T(128)}) all-reduce(f32[14852]{0:T(1024)S(1)} %concatenate.40, f32[]{:T(128)S(6)} %add.447), channel_id=1, replica_groups=mesh['dp'=4,'ctx'=8] {'dp','ctx'}, use_global_device_ids=true, to_apply=%region_48.50 | all-reduce | flops 14853 | bytes 118824 | tf_op jit(solution)/shard_map/psum | solution.py:352
  1116.7 2.6 multiply_subtract_fusion.1
  (731 shorter events, 234.2 us)
Async XLA Ops:
  7.2 84.0 %all-gather.11.cloned.1.call-start = ((), (), s32[]{:S(2)}) async-start(), calls=%async_computation | async-start | bytes 8650752 | tf_op jit(solution)/shard_map/all_gather | solution.py:271
  9.1 174.6 %all-gather.13.cloned.1.call-start = ((), (), s32[]{:S(2)}) async-start(), calls=%async_computation.1 | async-start | bytes 8921088 | tf_op jit(solution)/shard_map/all_gather | solution.py:272
  10.9 197.1 %all-gather.15.cloned.1.call-start = ((), (), s32[]{:S(2)}) async-start(), calls=%async_computation.2 | async-start | bytes 2359296 | tf_op jit(solution)/shard_map/all_gather | solution.py:36
  11.6 86.1 %copy-start.28 = (f32[1024,4]{1,0:T(8,128)}, f32[1024,4]{1,0:T(8,128)S(1)}, u32[]{:S(2)}) copy-start(f32[1024,4]{1,0:T(8,128)S(1)} %reshape.844) | copy-start | bytes 49156
  11.7 96.3 %copy-start.95 = (f32[128]{0:T(128)}, f32[128]{0:T(128)S(1)}, u32[]{:S(2)}) copy-start(f32[128]{0:T(128)S(1)} %fusion.309) | copy-start | bytes 1540
  11.8 85.9 %copy-start.121 = (f32[2]{0:T(128)}, f32[2]{0:T(128)S(1)}, u32[]{:S(2)}) copy-start(f32[2]{0:T(128)S(1)} %get-tuple-element.2850) | copy-start | bytes 28
  11.8 85.9 %copy-start.123 = (f32[2]{0:T(128)}, f32[2]{0:T(128)S(1)}, u32[]{:S(2)}) copy-start(f32[2]{0:T(128)S(1)} %get-tuple-element.2851) | copy-start | bytes 28
  12.4 95.6 %copy-start.69 = (f32[1024]{0:T(1024)}, f32[1024]{0:T(1024)S(1)}, u32[]{:S(2)}) copy-start(f32[1024]{0:T(1024)S(1)} %get-tuple-element.2845) | copy-start | bytes 12292
  13.0 84.7 %copy-start.98 = (f32[128,4]{0,1:T(4,128)}, f32[128,4]{0,1:T(4,128)S(1)}, u32[]{:S(2)}) copy-start(f32[128,4]{0,1:T(4,128)S(1)} %fusion.282) | copy-start | bytes 6148
  13.6 102.3 %copy-start.113 = (f32[128,2]{0,1:T(2,128)}, f32[128,2]{0,1:T(2,128)S(1)}, u32[]{:S(2)}) copy-start(f32[128,2]{0,1:T(2,128)S(1)} %get-tuple-element.2853) | copy-start | bytes 3076
  13.7 103.1 %copy-start.77 = (f32[2048]{0:T(1024)}, f32[2048]{0:T(1024)S(1)}, u32[]{:S(2)}) copy-start(f32[2048]{0:T(1024)S(1)} %get-tuple-element.2846) | copy-start | bytes 24580
  13.7 103.1 %copy-start.79 = (f32[2048]{0:T(1024)}, f32[2048]{0:T(1024)S(1)}, u32[]{:S(2)}) copy-start(f32[2048]{0:T(1024)S(1)} %get-tuple-element.2847) | copy-start | bytes 24580
  13.7 103.1 %copy-start.81 = (f32[2048]{0:T(1024)}, f32[2048]{0:T(1024)S(1)}, u32[]{:S(2)}) copy-start(f32[2048]{0:T(1024)S(1)} %get-tuple-element.2848) | copy-start | bytes 24580
  13.7 103.1 %copy-start.83 = (f32[2048]{0:T(1024)}, f32[2048]{0:T(1024)S(1)}, u32[]{:S(2)}) copy-start(f32[2048]{0:T(1024)S(1)} %get-tuple-element.2849) | copy-start | bytes 24580
  113.0 5.4 copy-start.15
  113.0 3.7 collective-permute-start
  162.5 77.1 %all-gather.17.cloned.1.call-start = ((), (), s32[]{:S(2)}) async-start(), calls=%async_computation.3 | async-start | bytes 4718592 | tf_op jit(solution)/shard_map/all_gather | solution.py:36
  164.6 277.5 %all-gather.19.cloned.1.call-start = ((), (), s32[]{:S(2)}) async-start(), calls=%async_computation.4 | async-start | bytes 2359296 | tf_op jit(solution)/shard_map/all_gather | solution.py:61
  183.3 271.7 %all-gather.21.cloned.1.call-start = ((), (), s32[]{:S(2)}) async-start(), calls=%async_computation.5 | async-start | bytes 4718592 | tf_op jit(solution)/shard_map/all_gather | solution.py:61
  258.1 7.0 copy-start.62
  284.2 7.0 copy-start.62
  309.4 5.8 copy-start.12
  313.3 7.9 copy-start.3
  313.3 7.9 copy-start.5
  343.4 5.1 copy-start.73
  344.9 5.1 copy-start.93
  344.9 5.1 copy-start.131
  373.1 5.1 copy-start.73
  390.2 6.9 slice-start
  418.3 649.8 %all-reduce.22.cloned.1.call-start = ((), (), s32[]{:S(2)}) async-start(), calls=%async_computation.6 | async-start | bytes 68157440
  431.1 8.4 copy-start.26
  431.1 8.3 copy-start.39
  455.2 16.9 %copy-start.42 = (pred[64,64]{1,0:T(8,128)(4,1)S(1)}, pred[64,64]{1,0:T(8,128)(4,1)}, u32[]{:S(2)}) copy-start(pred[64,64]{1,0:T(8,128)(4,1)} %get-tuple-element.3960) | copy-start | bytes 12292
  455.2 16.9 %copy-start.87 = (f32[2,2,64]{2,1,0:T(2,128)S(1)}, f32[2,2,64]{2,1,0:T(2,128)}, u32[]{:S(2)}) copy-start(f32[2,2,64]{2,1,0:T(2,128)} %get-tuple-element.3846) | copy-start | bytes 3076
  455.2 16.9 %copy-start.90 = (f32[2,2,64]{2,1,0:T(2,128)S(1)}, f32[2,2,64]{2,1,0:T(2,128)}, u32[]{:S(2)}) copy-start(f32[2,2,64]{2,1,0:T(2,128)} %get-tuple-element.3848) | copy-start | bytes 3076
  455.2 16.9 %copy-start.104 = (f32[2,2,64,1]{2,1,3,0:T(2,128)S(1)}, f32[2,2,64,1]{2,1,3,0:T(2,128)}, u32[]{:S(2)}) copy-start(f32[2,2,64,1]{2,1,3,0:T(2,128)} %get-tuple-element.3843) | copy-start | bytes 3076
  455.2 16.9 %copy-start.107 = (f32[2,2,64,1]{2,1,3,0:T(2,128)S(1)}, f32[2,2,64,1]{2,1,3,0:T(2,128)}, u32[]{:S(2)}) copy-start(f32[2,2,64,1]{2,1,3,0:T(2,128)} %get-tuple-element.3842) | copy-start | bytes 3076
  539.1 5.3 copy-start.47
  546.1 3.1 collective-permute-start.1
  575.5 540.5 %copy-start.91 = (f32[14852]{0:T(1024)S(1)}, f32[14852]{0:T(1024)}, u32[]{:S(2)}) copy-start(f32[14852]{0:T(1024)} %param.38) | copy-start | bytes 178228
  575.5 540.5 %copy-start.92 = (f32[14852]{0:T(1024)S(1)}, f32[14852]{0:T(1024)}, u32[]{:S(2)}) copy-start(f32[14852]{0:T(1024)} %param.39) | copy-start | bytes 178228
  575.7 541.0 %copy-start.50 = (f32[131072]{0:T(1024)S(1)}, f32[131072]{0:T(1024)}, u32[]{:S(2)}) copy-start(f32[131072]{0:T(1024)} %param.31) | copy-start | bytes 1572868
  1069.9 49.4 %copy-start.44 = (f32[131072]{0:T(1024)}, f32[131072]{0:T(1024)S(1)}, u32[]{:S(2)}) copy-start(f32[131072]{0:T(1024)S(1)} %get-tuple-element.2774) | copy-start | bytes 1572868
  1071.9 47.4 %copy-start.41 = (f32[135168]{0:T(1024)}, f32[135168]{0:T(1024)S(1)}, u32[]{:S(2)}) copy-start(f32[135168]{0:T(1024)S(1)} %get-tuple-element.2772) | copy-start | bytes 1622020
  1114.0 6.8 copy-start.64
  1114.0 5.3 copy-start.40
  1114.0 5.3 copy-start.60
  1114.0 5.3 copy-start.61
  (135 other events, 369.7 us)
Sparse Core Ops, SparseCore 0:
  11.4 79.7 all-gather.10
  94.7 76.8 all-gather.12
  174.1 26.4 all-gather.14
  203.0 36.5 all-gather.16
  241.3 27.8 all-gather.18
  418.4 36.6 all-gather.20
  565.2 502.9 all-reduce.21
where the time goes:
time: 1140 us; the launch traced here: 1130 us
  waiting for transfers between devices  615 us (54%)
  other arithmetic  166 us (15%)
  matrix products  152 us (13%)
  local copies, waits for them, and re-layouts  120 us (11%)
  blocking collectives  40.8 us (4%)
  between operations  18.7 us (2%)
  loops' own time  12 us (1%)
    unnamed x8, waiting for transfers between devices  492 us
    another operation x34, other arithmetic, group_parts(): jax.scipy.linalg.solve_triangular(system, right_side, lower=True, unit_di...  86.5 us
    all_gather x1, waiting for transfers between devices, body(): lax.all_gather(mix_part, ('dp', 'ctx'), axis=0, tiled=True)  77.5 us
    psum x1, blocking collectives, body(): lax.psum((small_local, shard_squares), ('dp', 'ctx'))  40.8 us
    dot_general x17, matrix products, combine(): jnp.einsum('hij,hjk->hik', second_map, first_shift, precision=HIGHEST)  32.5 us
    all_gather x2, waiting for transfers between devices, entering(): lax.all_gather(part.astype(kind), axis)  31.5 us
  transfers between devices with their start and end apart: 9, of which 5 were waited for; matrix products, arithmetic and copies ran while one was open for 28% of the time, Pallas kernels for 0%

commit v1 on v0

v1 whole, which is shorter than its diff:
```python
import math
import jax
import jax.numpy as jnp
from jax import lax
from jax.experimental import pallas as pl
from jax.experimental.pallas import tpu as pltpu
from jax.sharding import PartitionSpec as P

D = 1024
H = 2
DK = 256
DV = 512
FF = 1408
CONV = 4
GROUP = 64


EPSILON = 1e-06
ADAM_EPS = 1e-08
LEARN_RATE = 0.02
BETA_ONE = 0.9
BETA_TWO = 0.999
DECAY_RATE = 0.1
CORRECT_ONE = 1.0 - 0.9**3
CORRECT_TWO = 1.0 - 0.999**3
MAX_NORM = 1.0
HIGHEST = lax.Precision.HIGHEST


def from_behind(value, axis, steps):
    count = lax.axis_size(axis)
    initial, last = (max(0, -steps), min(count, count - steps))
    return lax.ppermute(value, axis, [(source, source + steps) for source in range(initial, last)])


def norm_scale(values, gain):
    return values * lax.rsqrt(jnp.mean(values * values, axis=-1, keepdims=True) + EPSILON) * gain


def swiglu(gate_part, up_part):
    return jax.nn.silu(gate_part) * up_part


def unpack_small(packed):
    width = 2 * H * DK + H * DV
    lengths = [D, D, DV, CONV * width, D * 2 * H, H, H]
    pieces = []
    offset = 0
    for length in lengths:
        pieces.append(packed[offset : offset + length])
        offset = offset + length
    return (
        pieces[0],
        pieces[1],
        pieces[2],
        pieces[3].reshape(CONV, width),
        pieces[4].reshape(D, 2 * H),
        pieces[5],
        pieces[6],
    )


def split_weights(mix_whole, ffn_whole):
    mix_rows = mix_whole.reshape(-1, D)
    ffn_rows = ffn_whole.reshape(-1, D)
    edge = 2 * H * DK + 2 * H * DV
    return (mix_rows[:edge], mix_rows[edge:], ffn_rows[: 2 * FF], ffn_rows[2 * FF :])


PAD = 16
HIGH = dict(precision=HIGHEST, preferred_element_type=jnp.float32)


def mm(a, b):
    return lax.dot_general(a, b, (((1,), (0,)), ((), ())), **HIGH)


def mm_nt(a, b):
    return lax.dot_general(a, b, (((1,), (1,)), ((), ())), **HIGH)


def mm_tn(a, b):
    return lax.dot_general(a, b, (((0,), (0,)), ((), ())), **HIGH)


def halves(a):
    high = a.astype(jnp.bfloat16)
    return high, (a - high.astype(jnp.float32)).astype(jnp.bfloat16)


def wire_mm(a, b, dims):
    high, low = halves(b)
    first = lax.dot_general(a, high, (dims, ((), ())), preferred_element_type=jnp.float32)
    return first + lax.dot_general(a, low, (dims, ((), ())), preferred_element_type=jnp.float32)


def iotas(size):
    shape = (size, size)
    return (
        lax.broadcasted_iota(jnp.int32, shape, 0),
        lax.broadcasted_iota(jnp.int32, shape, 1),
    )


def to_row(column, rows, cols):
    return jnp.sum(jnp.where(rows == cols, column, 0.0), axis=0, keepdims=True)


def unit_inverse(strict_part, rows, cols):
    size = strict_part.shape[0]
    inverse = jnp.where(rows == cols, 1.0, 0.0) - jnp.where(
        (rows // 2 == cols // 2), strict_part, 0.0
    )
    block = 2
    while block < size:
        joined = (rows // (2 * block) == cols // (2 * block)) & (rows // block != cols // block)
        off = jnp.where(joined, strict_part, 0.0)
        inverse = inverse - mm(mm(inverse, off), inverse)
        block = 2 * block
    return inverse


def silu_pair(x):
    gate = jax.nn.sigmoid(x)
    return x * gate, gate * (1.0 + x * (1.0 - gate))


def conv_sum(extended_ref, taps, count):
    total = None
    for tap in range(CONV):
        piece = taps[tap : tap + 1] * extended_ref[pl.ds(8 - (CONV - 1) + tap, count), :]
        total = piece if total is None else total + piece
    return total


def unit_rows(part):
    return lax.rsqrt(jnp.sum(part * part, axis=-1, keepdims=True) + EPSILON)


def decay_terms(decay_column, rows, cols):
    lower = rows >= cols
    size = rows.shape[0]
    spread_in = jnp.broadcast_to(decay_column, (size, 128))
    cumulative = mm(jnp.where(lower, 1.0, 0.0), spread_in)[:, :1]
    across = to_row(cumulative, rows, cols)
    matrix = jnp.where(lower, jnp.exp(jnp.where(lower, cumulative - across, 0.0)), 0.0)
    last = cumulative[size - 1 : size]
    return matrix, jnp.exp(cumulative), jnp.exp(last - cumulative), jnp.exp(last)


def forward_parts(
    projected_ref, border_ref, taps_ref, beta_ref, decay_ref,
    wire_ref, query_ref, keys_ref, values_ref, inverse_ref, extended_ref,
):
    count = projected_ref.shape[0]
    width = taps_ref.shape[1]
    extended_ref[0:8, :] = border_ref[...]
    extended_ref[pl.ds(8, count), :] = projected_ref[:, :width]
    summed = conv_sum(extended_ref, taps_ref[...], count)
    activated = summed * jax.nn.sigmoid(summed)
    rows, cols = iotas(count)
    for head in range(H):
        query_part = activated[:, head * DK : (head + 1) * DK]
        key_part = activated[:, (H + head) * DK : (H + head + 1) * DK]
        start = 2 * H * DK + head * DV
        values = activated[:, start : start + DV]
        query = query_part * unit_rows(query_part) * DK ** (-0.5)
        keys = key_part * unit_rows(key_part)
        beta = beta_ref[:, head : head + 1]
        matrix, grown, to_end, whole = decay_terms(decay_ref[:, head : head + 1], rows, cols)
        system = jnp.where(rows > cols, beta * mm_nt(keys, keys) * matrix, 0.0)
        inverse = unit_inverse(system, rows, cols)
        key_mix = mm(inverse, keys * (beta * grown))
        value_mix = mm(inverse, values * beta)
        base = head * (2 * DK + DV)
        wire_ref[0:count, base : base + DK] = (keys * to_end).astype(jnp.bfloat16)
        wire_ref[0:count, base + DK : base + 2 * DK] = key_mix.astype(jnp.bfloat16)
        wire_ref[0:count, base + 2 * DK : base + 2 * DK + DV] = value_mix.astype(jnp.bfloat16)
        high, low = halves(jnp.broadcast_to(whole, (PAD, 2 * DK + DV)))
        first = lax.broadcasted_iota(jnp.int32, (PAD, 2 * DK + DV), 0) < 8
        tail = jnp.where(first, high.astype(jnp.float32), low.astype(jnp.float32))
        wire_ref[pl.ds(count, PAD), base : base + 2 * DK + DV] = tail.astype(jnp.bfloat16)
        query_ref[:, head * DK : (head + 1) * DK] = query
        keys_ref[:, head * DK : (head + 1) * DK] = keys
        values_ref[:, head * DV : (head + 1) * DV] = values
        inverse_ref[head] = inverse


def wire_parts(wire_ref, index, head, count):
    base = head * (2 * DK + DV)
    to_end = wire_ref[index, 0:count, base : base + DK]
    key_mix = wire_ref[index, 0:count, base + DK : base + 2 * DK]
    value_mix = wire_ref[index, 0:count, base + 2 * DK : base + 2 * DK + DV]
    tail = wire_ref[index, pl.ds(count, PAD), base : base + 128].astype(jnp.float32)
    whole = tail[0:1, 0:1] + tail[8:9, 0:1]
    return to_end, key_mix, value_mix, whole


def own_mix(inverse, keys, values, beta, grown):
    return mm(inverse, keys * (beta * grown)), mm(inverse, values * beta)


def forward_chain(
    place_ref, wire_ref, query_ref, keys_ref, values_ref, inverse_ref, beta_ref, decay_ref,
    gate_ref, gain_ref, head_out_ref, mixed_ref, state_ref, pseudo_ref,
):
    count = query_ref.shape[0]
    state_ref[...] = jnp.zeros_like(state_ref)

    def lap(index, carry):
        for head in range(H):
            to_end, key_mix, value_mix, whole = wire_parts(wire_ref, index, head, count)
            state = state_ref[head]
            pseudo = value_mix.astype(jnp.float32) - wire_mm(key_mix, state, ((1,), (0,)))
            state_ref[head] = whole * state + wire_mm(to_end, pseudo, ((0,), (0,)))
        return carry

    lax.fori_loop(0, place_ref[0], lap, 0)
    rows, cols = iotas(count)
    for head in range(H):
        query = query_ref[:, head * DK : (head + 1) * DK]
        keys = keys_ref[:, head * DK : (head + 1) * DK]
        span = slice(head * DV, (head + 1) * DV)
        beta = beta_ref[:, head : head + 1]
        matrix, grown, to_end, whole = decay_terms(decay_ref[:, head : head + 1], rows, cols)
        key_mix, value_mix = own_mix(inverse_ref[head], keys, values_ref[:, span], beta, grown)
        state = state_ref[head]
        pseudo = value_mix - mm(key_mix, state)
        mixed = mm(query * grown, state) + mm(mm_nt(query, keys) * matrix, pseudo)
        scale = lax.rsqrt(jnp.mean(mixed * mixed, axis=-1, keepdims=True) + EPSILON)
        gated, unused = silu_pair(gate_ref[:, span])
        head_out_ref[:, span] = (mixed * scale * gain_ref[...] * gated).astype(jnp.bfloat16)
        mixed_ref[:, span] = mixed
        pseudo_ref[:, span] = pseudo


def backward_local(
    grad_ref, mixed_ref, query_ref, keys_ref, values_ref, inverse_ref, beta_ref, decay_ref,
    gate_ref, gain_ref, local_ref, grad_mixed_ref, grad_gate_ref, grad_gain_ref,
):
    count = query_ref.shape[0]
    rows, cols = iotas(count)
    gain_total = jnp.zeros((1, DV), jnp.float32)
    for head in range(H):
        query = query_ref[:, head * DK : (head + 1) * DK]
        keys = keys_ref[:, head * DK : (head + 1) * DK]
        span = slice(head * DV, (head + 1) * DV)
        mixed = mixed_ref[:, span]
        grad = grad_ref[:, span]
        scale = lax.rsqrt(jnp.mean(mixed * mixed, axis=-1, keepdims=True) + EPSILON)
        plain = mixed * scale
        gated, slope = silu_pair(gate_ref[:, span])
        grad_gate_ref[:, span] = grad * plain * gain_ref[...] * slope
        grad_normed = grad * gated
        gain_total = gain_total + jnp.sum(grad_normed * plain, axis=0, keepdims=True)
        pulled = grad_normed * gain_ref[...]
        grad_mixed = scale * (pulled - plain * jnp.mean(pulled * plain, axis=-1, keepdims=True))
        grad_mixed_ref[:, span] = grad_mixed
        beta = beta_ref[:, head : head + 1]
        matrix, grown, to_end, whole = decay_terms(decay_ref[:, head : head + 1], rows, cols)
        key_mix = mm(inverse_ref[head], keys * (beta * grown))
        grad_pseudo = mm_tn(mm_nt(query, keys) * matrix, grad_mixed)
        local = mm_tn(query * grown, grad_mixed) - mm_tn(key_mix, grad_pseudo)
        local_ref[head * DK : (head + 1) * DK, :] = local.astype(jnp.bfloat16)
    grad_gain_ref[...] = gain_total


def backward_chain(
    place_ref, wire_ref, local_ref, query_ref, keys_ref, values_ref, inverse_ref, beta_ref,
    decay_ref, state_ref, pseudo_ref, grad_mixed_ref, projected_ref, border_ref, taps_ref,
    grad_conv_ref, grad_border_ref, grad_taps_ref, grad_beta_ref, grad_decay_ref,
    after_ref, extended_ref, padded_ref,
):
    count = query_ref.shape[0]
    width = taps_ref.shape[1]
    devices = wire_ref.shape[0]
    after_ref[...] = jnp.zeros_like(after_ref)

    def lap(step, carry):
        index = devices - 1 - step
        for head in range(H):
            to_end, key_mix, value_mix, whole = wire_parts(wire_ref, index, head, count)
            after = after_ref[head]
            inner = wire_mm(to_end, after, ((1,), (0,)))
            local = local_ref[index, head * DK : (head + 1) * DK, :].astype(jnp.float32)
            after_ref[head] = whole * after - wire_mm(key_mix, inner, ((0,), (0,))) + local
        return carry

    lax.fori_loop(0, devices - 1 - place_ref[0], lap, 0)
    extended_ref[0:8, :] = border_ref[...]
    extended_ref[pl.ds(8, count), :] = projected_ref[:, :width]
    taps = taps_ref[...]
    summed = conv_sum(extended_ref, taps, count)
    activated, slope = silu_pair(summed)
    padded_ref[0:8, :] = jnp.zeros((8, width), jnp.float32)
    padded_ref[pl.ds(8 + count, 8), :] = jnp.zeros((8, width), jnp.float32)
    rows, cols = iotas(count)
    lower = rows >= cols
    strict = rows > cols
    lanes = lax.broadcasted_iota(jnp.int32, (count, 128), 1)
    beta_out = jnp.zeros((count, 128), jnp.float32)
    cumulative_out = jnp.zeros((count, 128), jnp.float32)
    row_column = lax.broadcasted_iota(jnp.int32, (count, 1), 0)
    for head in range(H):
        query = query_ref[:, head * DK : (head + 1) * DK]
        keys = keys_ref[:, head * DK : (head + 1) * DK]
        span = slice(head * DV, (head + 1) * DV)
        values = values_ref[:, span]
        beta = beta_ref[:, head : head + 1]
        matrix, grown, to_end, whole = decay_terms(decay_ref[:, head : head + 1], rows, cols)
        inverse = inverse_ref[head]
        state = state_ref[head]
        after = after_ref[head]
        pseudo = pseudo_ref[:, span]
        grad_mixed = grad_mixed_ref[:, span]
        keys_grown = keys * (beta * grown)
        key_mix = mm(inverse, keys_grown)
        value_mix = mm(inverse, values * beta)
        gram = mm_nt(keys, keys)
        system = jnp.where(strict, beta * gram * matrix, 0.0)
        scores = mm_nt(query, keys) * matrix
        keys_end = keys * to_end
        query_grown = query * grown
        grad_query_grown = mm_nt(grad_mixed, state)
        grad_scores = jnp.where(lower, mm_nt(grad_mixed, pseudo), 0.0)
        grad_pseudo = mm_tn(scores, grad_mixed) + mm(keys_end, after)
        grad_keys_end = mm_nt(pseudo, after)
        grad_whole = jnp.sum(jnp.sum(after * state, axis=1, keepdims=True), axis=0, keepdims=True)
        grad_value_in = mm_tn(inverse, grad_pseudo)
        grad_key_in = mm_tn(inverse, -mm_nt(grad_pseudo, state))
        grad_system = -jnp.where(
            strict, mm_nt(grad_value_in, value_mix) + mm_nt(grad_key_in, key_mix), 0.0
        )
        grad_raw = grad_scores * matrix
        grad_query = mm(grad_raw, keys) + grad_query_grown * grown
        grad_keys = mm_tn(grad_raw, query)
        weighted = grad_system * matrix
        grad_beta = jnp.sum(weighted * gram, axis=1, keepdims=True)
        grad_gram = weighted * beta
        grad_keys = grad_keys + mm(grad_gram, keys) + mm_tn(grad_gram, keys)
        spread = grad_scores * scores + grad_system * system
        grad_cumulative = jnp.sum(spread, axis=1, keepdims=True)
        across = jnp.sum(spread, axis=0, keepdims=True)
        grad_cumulative = grad_cumulative - jnp.sum(
            jnp.where(rows == cols, across, 0.0), axis=1, keepdims=True
        )
        grad_keys = grad_keys + grad_key_in * (beta * grown)
        through = jnp.sum(grad_key_in * keys, axis=1, keepdims=True) * grown
        grad_beta = grad_beta + through + jnp.sum(grad_value_in * values, axis=1, keepdims=True)
        grad_cumulative = grad_cumulative + through * beta
        grad_values = grad_value_in * beta
        grad_cumulative = grad_cumulative + jnp.sum(
            grad_query_grown * query_grown, axis=1, keepdims=True
        )
        grad_keys = grad_keys + grad_keys_end * to_end
        ending = jnp.sum(grad_keys_end * keys_end, axis=1, keepdims=True)
        final = jnp.sum(ending, axis=0, keepdims=True) + whole * grad_whole
        grad_cumulative = grad_cumulative - ending + jnp.where(row_column == count - 1, final, 0.0)
        beta_out = jnp.where(lanes == head, grad_beta, beta_out)
        cumulative_out = jnp.where(lanes == head, grad_cumulative, cumulative_out)
        key_part = activated[:, (H + head) * DK : (H + head + 1) * DK]
        key_scale = unit_rows(key_part)
        query_part = activated[:, head * DK : (head + 1) * DK]
        query_scale = unit_rows(query_part)
        factor = DK ** (-0.5)
        grad_query_part = (factor * query_scale) * (
            grad_query
            - query_part
            * (query_scale * query_scale)
            * jnp.sum(grad_query * query_part, axis=-1, keepdims=True)
        )
        grad_key_part = key_scale * (
            grad_keys
            - key_part
            * (key_scale * key_scale)
            * jnp.sum(grad_keys * key_part, axis=-1, keepdims=True)
        )
        spots = (head * DK, (H + head) * DK, 2 * H * DK + head * DV)
        for spot, grad in zip(spots, (grad_query_part, grad_key_part, grad_values)):
            size = grad.shape[1]
            padded_ref[pl.ds(8, count), spot : spot + size] = grad * slope[:, spot : spot + size]
    grad_beta_ref[...] = beta_out
    grad_decay_ref[...] = mm_tn(jnp.where(lower, 1.0, 0.0), cumulative_out)
    conv_total = jnp.zeros((count, width), jnp.float32)
    border_total = jnp.zeros((8, width), jnp.float32)
    summed_grad = padded_ref[pl.ds(8, count), :]
    tap_rows = lax.broadcasted_iota(jnp.int32, (8, width), 0)
    taps_total = jnp.zeros((8, width), jnp.float32)
    for tap in range(CONV):
        shift = CONV - 1 - tap
        conv_total = conv_total + taps[tap : tap + 1] * padded_ref[pl.ds(8 + shift, count), :]
        border_total = border_total + taps[tap : tap + 1] * padded_ref[pl.ds(shift, 8), :]
        piece = jnp.sum(
            summed_grad * extended_ref[pl.ds(8 - (CONV - 1) + tap, count), :],
            axis=0,
            keepdims=True,
        )
        taps_total = jnp.where(tap_rows == tap, piece, taps_total)
    grad_conv_ref[...] = conv_total
    grad_border_ref[...] = border_total
    grad_taps_ref[...] = taps_total


def fused(body, outputs, scratch=(), scalars=0, cost=(0, 0), label=None):
    def call(*args):
        vmem = pl.BlockSpec(memory_space=pltpu.VMEM)
        smem = pl.BlockSpec(memory_space=pltpu.SMEM)
        return pl.pallas_call(
            body,
            out_shape=outputs,
            in_specs=[smem] * scalars + [vmem] * (len(args) - scalars),
            out_specs=[vmem] * len(outputs),
            scratch_shapes=list(scratch),
            compiler_params=pltpu.CompilerParams(vmem_limit_bytes=60 * 2**20),
            cost_estimate=pl.CostEstimate(
                flops=cost[0], bytes_accessed=cost[1], transcendentals=0
            ),
            name=label,
        )(*args)

    return call


def gates(gate_logits, a_log, dt_bias):
    beta = jax.nn.sigmoid(gate_logits[:, :H])
    decay = -jnp.exp(a_log) * jax.nn.softplus(gate_logits[:, H:] + dt_bias)
    return beta, decay


def scatter_rows(pieces):
    outer, inner = lax.axis_size("dp"), lax.axis_size("ctx")
    whole = jnp.concatenate([piece.astype(jnp.bfloat16) for piece in pieces], axis=0)
    lane = math.gcd(whole.size // (outer * inner), D)
    blocks = whole.reshape(outer, inner, -1, lane)
    part = lax.psum_scatter(blocks, "ctx", scatter_dimension=1, tiled=False)
    own = lax.psum_scatter(part, "dp", scatter_dimension=0, tiled=False)
    return own.astype(jnp.float32).reshape(-1)


def adam_step(weight, grad_full, first, second, clip):
    grad_clipped = grad_full * clip
    first_new = BETA_ONE * first + (1.0 - BETA_ONE) * grad_clipped
    second_new = BETA_TWO * second + (1.0 - BETA_TWO) * grad_clipped * grad_clipped
    update = (
        first_new / CORRECT_ONE / (jnp.sqrt(second_new / CORRECT_TWO) + ADAM_EPS)
        + DECAY_RATE * weight
    )
    return (weight - LEARN_RATE * update, first_new, second_new)


def body(
    inputs,
    cotangent,
    mixer_params,
    mixer_first,
    mixer_second,
    ffn_params,
    ffn_first,
    ffn_second,
    small_params,
    small_first,
    small_second,
):
    gain_one, gain_two, gain_head, tap_values, w_gates, a_log, dt_bias = unpack_small(small_params)
    width = tap_values.shape[1]
    mix_part = mixer_params.astype(jnp.bfloat16)
    ffn_part = ffn_params.astype(jnp.bfloat16)
    mix_whole, ffn_whole = (
        lax.all_gather(mix_part, ("dp", "ctx"), axis=0, tiled=True),
        lax.all_gather(ffn_part, ("dp", "ctx"), axis=0, tiled=True),
    )
    w_in, w_out, w_ffn, w_down = split_weights(mix_whole, ffn_whole)
    x_float = inputs[0].astype(jnp.float32)
    count = x_float.shape[0]
    normed_in = norm_scale(x_float, gain_one).astype(jnp.bfloat16)
    projected = jnp.dot(normed_in, w_in.T, preferred_element_type=jnp.float32)
    gate_logits = jnp.dot(normed_in.astype(jnp.float32), w_gates, precision=HIGHEST)
    f32 = jnp.float32
    devices = lax.axis_size("ctx")
    place = lax.axis_index("ctx").astype(jnp.int32).reshape(1)
    out_gate = projected[:, width:]
    edge = from_behind(projected[count - 8 :, :width], "ctx", 1)
    border = jnp.where(lax.broadcasted_iota(jnp.int32, (8, 1), 0) >= 8 - (CONV - 1), edge, 0.0)
    (beta, decay), pull_gates = jax.vjp(gates, gate_logits, a_log, dt_bias)
    wire, query, keys, values, inverse = fused(
        forward_parts,
        (
            jax.ShapeDtypeStruct((count + PAD, H * (2 * DK + DV)), jnp.bfloat16),
            jax.ShapeDtypeStruct((count, H * DK), f32),
            jax.ShapeDtypeStruct((count, H * DK), f32),
            jax.ShapeDtypeStruct((count, H * DV), f32),
            jax.ShapeDtypeStruct((H, count, count), f32),
        ),
        scratch=(pltpu.VMEM((count + 8, width), f32),),
        label="forward_parts",
    )(projected, border, tap_values, beta, decay)
    wires = lax.all_gather(wire, "ctx")
    gain_row = gain_head.reshape(1, DV)
    head_out, mixed, state, pseudo = fused(
        forward_chain,
        (
            jax.ShapeDtypeStruct((count, H * DV), jnp.bfloat16),
            jax.ShapeDtypeStruct((count, H * DV), f32),
            jax.ShapeDtypeStruct((H, DK, DV), f32),
            jax.ShapeDtypeStruct((count, H * DV), f32),
        ),
        scalars=1,
        label="forward_chain",
    )(place, wires, query, keys, values, inverse, beta, decay, out_gate, gain_row)
    resid = x_float + jnp.dot(head_out, w_out, preferred_element_type=jnp.float32)
    normed_mid = norm_scale(resid, gain_two).astype(jnp.bfloat16)
    ffn_pre = jnp.dot(normed_mid, w_ffn.T, preferred_element_type=jnp.float32)
    gate_part = ffn_pre[:, :FF]
    up_part = ffn_pre[:, FF:]
    hidden_act = swiglu(gate_part, up_part).astype(jnp.bfloat16)
    result = (resid + jnp.dot(hidden_act, w_down, preferred_element_type=jnp.float32)).astype(
        jnp.bfloat16
    )
    seq_grad = cotangent[0]
    grad_float = seq_grad.astype(jnp.float32)
    grad_down = jnp.dot(hidden_act.T, seq_grad, preferred_element_type=jnp.float32)
    grad_hidden = jnp.dot(seq_grad, w_down.T, preferred_element_type=jnp.float32)
    unused_one, pull_swiglu = jax.vjp(swiglu, gate_part, up_part)
    grad_gate, grad_up = pull_swiglu(grad_hidden)
    grad_pre = jnp.concatenate([grad_gate, grad_up], axis=1).astype(jnp.bfloat16)
    grad_ffn = jnp.dot(grad_pre.T, normed_mid, preferred_element_type=jnp.float32)
    grad_mid = jnp.dot(grad_pre, w_ffn, preferred_element_type=jnp.float32)
    unused_two, pull_mid = jax.vjp(norm_scale, resid, gain_two)
    grad_through, grad_gain_two = pull_mid(grad_mid)
    grad_resid = grad_float + grad_through
    resid_half = grad_resid.astype(jnp.bfloat16)
    grad_out = jnp.dot(head_out.T, resid_half, preferred_element_type=jnp.float32)
    grad_head = jnp.dot(resid_half, w_out.T, preferred_element_type=jnp.float32)
    local, grad_mixed, grad_gate_out, grad_gain_head = fused(
        backward_local,
        (
            jax.ShapeDtypeStruct((H * DK, DV), jnp.bfloat16),
            jax.ShapeDtypeStruct((count, H * DV), f32),
            jax.ShapeDtypeStruct((count, H * DV), f32),
            jax.ShapeDtypeStruct((1, DV), f32),
        ),
        label="backward_local",
    )(grad_head, mixed, query, keys, values, inverse, beta, decay, out_gate, gain_row)
    locals_all = lax.all_gather(local, "ctx")
    locals_all, grad_ffn, grad_down = lax.optimization_barrier((locals_all, grad_ffn, grad_down))
    ffn_shard = scatter_rows((grad_ffn, grad_down))
    grad_conv, grad_border, grad_taps, grad_beta, grad_decay = fused(
        backward_chain,
        (
            jax.ShapeDtypeStruct((count, width), f32),
            jax.ShapeDtypeStruct((8, width), f32),
            jax.ShapeDtypeStruct((8, width), f32),
            jax.ShapeDtypeStruct((count, 128), f32),
            jax.ShapeDtypeStruct((count, 128), f32),
        ),
        scratch=(
            pltpu.VMEM((H, DK, DV), f32),
            pltpu.VMEM((count + 8, width), f32),
            pltpu.VMEM((count + 16, width), f32),
        ),
        scalars=1,
        label="backward_chain",
    )(
        place, wires, locals_all, query, keys, values, inverse, beta, decay, state, pseudo,
        grad_mixed, projected, border, tap_values,
    )
    grad_logits, grad_alog, grad_bias = pull_gates((grad_beta[:, :H], grad_decay[:, :H]))
    returned = from_behind(grad_border, "ctx", -1)[8 - (CONV - 1) :]
    grad_conv = grad_conv.at[count - (CONV - 1) :].add(returned)
    grad_proj = jnp.concatenate([grad_conv, grad_gate_out], axis=1).astype(jnp.bfloat16)
    grad_in = jnp.dot(grad_proj.T, normed_in, preferred_element_type=jnp.float32)
    grad_normed = jnp.dot(grad_proj, w_in, preferred_element_type=jnp.float32) + jnp.dot(
        grad_logits, w_gates.T, precision=HIGHEST
    )
    grad_gates = jnp.dot(normed_in.astype(jnp.float32).T, grad_logits, precision=HIGHEST)
    unused_six, pull_in = jax.vjp(norm_scale, x_float, gain_one)
    grad_x, grad_gain_one = pull_in(grad_normed)
    grad_input = (grad_resid + grad_x).astype(jnp.bfloat16)
    small_local = jnp.concatenate(
        [
            grad_gain_one,
            grad_gain_two,
            grad_gain_head.reshape(-1),
            grad_taps[:CONV].reshape(-1),
            grad_gates.reshape(-1),
            grad_alog,
            grad_bias,
        ]
    )
    small_grad = lax.psum(small_local, ("dp", "ctx"))
    ffn_shard, grad_in, grad_out = lax.optimization_barrier((ffn_shard, grad_in, grad_out))
    mix_shard = scatter_rows((grad_in, grad_out))
    small_grad, mix_shard = lax.optimization_barrier((small_grad, mix_shard))
    shard_squares = jnp.sum(mix_shard * mix_shard) + jnp.sum(ffn_shard * ffn_shard)
    total_squares = lax.psum(shard_squares, ("dp", "ctx"))
    squares = total_squares + jnp.sum(small_grad * small_grad)
    clip = jnp.minimum(1.0, MAX_NORM / (jnp.sqrt(squares) + 1e-06))
    mixer_new, mixer_first_new, mixer_second_new = adam_step(
        mixer_params, mix_shard, mixer_first, mixer_second, clip
    )
    ffn_new, ffn_first_new, ffn_second_new = adam_step(
        ffn_params, ffn_shard, ffn_first, ffn_second, clip
    )
    small_new, small_first_new, small_second_new = adam_step(
        small_params, small_grad, small_first, small_second, clip
    )
    return (
        result[None],
        grad_input[None],
        mix_shard,
        ffn_shard,
        small_grad,
        mixer_new,
        mixer_first_new,
        mixer_second_new,
        ffn_new,
        ffn_first_new,
        ffn_second_new,
        small_new,
        small_first_new,
        small_second_new,
    )


def solution(mesh):
    return jax.shard_map(
        body,
        mesh=mesh,
        in_specs=(
            P("dp", "ctx", None),
            P("dp", "ctx", None),
            P(("dp", "ctx")),
            P(("dp", "ctx")),
            P(("dp", "ctx")),
            P(("dp", "ctx")),
            P(("dp", "ctx")),
            P(("dp", "ctx")),
            P(),
            P(),
            P(),
        ),
        out_specs=(
            P("dp", "ctx", None),
            P("dp", "ctx", None),
            P(("dp", "ctx")),
            P(("dp", "ctx")),
            P(),
            P(("dp", "ctx")),
            P(("dp", "ctx")),
            P(("dp", "ctx")),
            P(("dp", "ctx")),
            P(("dp", "ctx")),
            P(("dp", "ctx")),
            P(),
            P(),
            P(),
        ),
        check_vma=False,
    )
```

time: 1140 us -> 737 us (0.65)
  waiting for transfers between devices: 615 us -> 399 us
  other arithmetic: 166 us -> 36.2 us
  matrix products: 152 us -> 39.8 us
  Pallas kernels: 0 us -> 46.5 us
  blocking collectives: 40.8 us -> 80.7 us
  local copies, waits for them, and re-layouts: 120 us -> 92.2 us
  loops' own time: 12 us -> 0 us
    unnamed x8 -> x10, waiting for transfers between devices: 492 us -> 250 us
    dot_general x79 -> x0, matrix products: 105 us -> none  [the longest x17 32.5 us: combine(): jnp.einsum('hij,hjk->hik', second_map, first_shift, precision=HIGHEST)]
    another operation x60 -> x2, other arithmetic: 90.4 us -> 3.07 us  [the longest x34 86.5 us: group_parts(): jax.scipy.linalg.solve_triangular(system, right_side, lower=True, unit_di...]
    pallas_call x0 -> x4, Pallas kernels: none -> 46.5 us  [call(): pl.pallas_call(body, out_shape=outputs, in_specs=[smem] * scalars + [vmem...]
    psum x1 -> x2, blocking collectives: 40.8 us -> 80.7 us  [the longest x1 40.5 us: body(): small_grad = lax.psum(small_local, ('dp', 'ctx'))]
    all_gather x1, waiting for transfers between devices: 0.02 us -> 36.6 us  [body(): lax.all_gather(ffn_part, ('dp', 'ctx'), axis=0, tiled=True)]
    reshape x14 -> x3, local copies, waits for them, and re-layouts: 3.68 us -> 25.8 us  [the longest x2 25.1 us: scatter_rows(): blocks = whole.reshape(outer, inner, -1, lane)]
    unnamed x198 -> x74, local copies, waits for them, and re-layouts: 21.3 us -> 3.49 us
  transfers between devices with their start and end apart: 9 -> 10, of which waited for: 5 -> 7; matrix products, arithmetic and copies ran while one was open for 28% -> 13% of each run, Pallas kernels for 0% -> 4%
where the time goes in v1:
time: 737 us; the launch traced here: 727 us
  waiting for transfers between devices  399 us (54%)
  local copies, waits for them, and re-layouts  92.2 us (13%)
  blocking collectives  80.7 us (11%)
  Pallas kernels  46.5 us (6%)
  matrix products  39.8 us (5%)
  other arithmetic  36.2 us (5%)
  between operations  17.7 us (2%)
  starting transfers between devices  15.2 us (2%)
    unnamed x10, waiting for transfers between devices  250 us
    all_gather x1, waiting for transfers between devices, body(): lax.all_gather(mix_part, ('dp', 'ctx'), axis=0, tiled=True)  72.7 us
    pallas_call x4, Pallas kernels, call(): pl.pallas_call(body, out_shape=outputs, in_specs=[smem] * scalars + [vmem...  46.5 us
    psum x1, blocking collectives, body(): small_grad = lax.psum(small_local, ('dp', 'ctx'))  40.5 us
    psum x1, blocking collectives, body(): total_squares = lax.psum(shard_squares, ('dp', 'ctx'))  40.2 us
    all_gather x1, waiting for transfers between devices, body(): lax.all_gather(ffn_part, ('dp', 'ctx'), axis=0, tiled=True)  36.6 us
    reshape x2, local copies, waits for them, and re-layouts, scatter_rows(): blocks = whole.reshape(outer, inner, -1, lane)  25.1 us
    all_gather x1, waiting for transfers between devices, body(): locals_all = lax.all_gather(local, 'ctx')  23.8 us
  transfers between devices with their start and end apart: 10, of which 7 were waited for; matrix products, arithmetic and copies ran while one was open for 13% of the time, Pallas kernels for 4%

profile of v1, /device:TPU:0, one launch (start us, length us, event | category | flops | bytes accessed | tf_op | source)
XLA Modules:
  0.0 727.4 jit_solution(2078643945249819705)
XLA Ops:
  7.2 1.8 convert_element_type.74
  9.1 1.8 convert_element_type.79
  18.6 72.7 %all-gather.7.cloned.1.call-done = bf16[4194304]{0:T(1024)(128)(2,1)} async-done(((bf16[131072]{0:T(1024)(128)(2,1)}), bf16[4194304]{0:T(1024)(128)(2,1)}) %all-gather.7.cloned.1.call-update) | async-done | bytes 8388624 | tf_op jit(solution)/shard_map/all_gather | solution.py:469
  91.2 6.5 slice.160
  97.8 10.4 %slice.136 = bf16[3072,1024]{1,0:T(8,128)(2,1)} reshape(bf16[3145728]{0:T(1024)(128)(2,1)} %slice.160) | data formatting | bytes 12582912 | tf_op jit(solution)/shard_map/slice | solution.py:67
  108.2 5.0 fusion.62.projected_ref
  113.2 2.2 collective-permute-start
  116.9 9.3 %forward_parts.1 = (bf16[144,2048]{1,0:T(8,128)(2,1)}, f32[128,512]{1,0:T(8,128)}, f32[128,512]{1,0:T(8,128)}, f32[128,1024]{1,0:T(8,128)}, f32[2,128,128]{2,1,0:T(8,128)}) custom-call(f32[128,3072]{1,0:T(8,128)} %copy-done, f32[8,2048]{1,0:T(8,128)} %broadcast_select_fusion.border_ref, f32[4,2048]{1,0:T(4,128)} %reshape.204.taps_ref, ...), custom_call_target="tpu_custom_call" | custom-call | tf_op jit(solution)/shard_map/forward_parts/pallas_call | solution.py:408
  126.9 1.9 slice.164.gate_ref
  128.8 3.1 slice.165
  132.0 2.8 slice.147
  134.8 36.6 %all-gather.9.cloned.1.call-done = bf16[4325376]{0:T(1024)(128)(2,1)} async-done(((bf16[135168]{0:T(1024)(128)(2,1)}), bf16[4325376]{0:T(1024)(128)(2,1)}) %all-gather.9.cloned.1.call-update) | async-done | bytes 8650768 | tf_op jit(solution)/shard_map/all_gather | solution.py:470
  171.4 6.1 slice.166
  177.6 9.7 %slice.150 = bf16[2816,1024]{1,0:T(8,128)(2,1)} reshape(bf16[2883584]{0:T(1024)(128)(2,1)} %slice.166) | data formatting | bytes 11534336 | tf_op jit(solution)/shard_map/slice | solution.py:67
  187.3 3.0 slice.169
  190.3 5.7 slice.154
  196.0 14.8 %all-gather.11.cloned.1.call-done = bf16[1152,2048]{1,0:T(8,128)(2,1)} async-done(((bf16[144,2048]{1,0:T(8,128)(2,1)}), bf16[1152,2048]{1,0:T(8,128)(2,1)}) %all-gather.11.cloned.1.call-update) | async-done | bytes 4718608 | tf_op jit(solution)/shard_map/all_gather | solution.py:497
  210.8 7.8 %forward_chain.1 = (bf16[128,1024]{1,0:T(8,128)(2,1)}, f32[128,1024]{1,0:T(8,128)}, f32[2,256,512]{2,1,0:T(8,128)}, f32[128,1024]{1,0:T(8,128)}) custom-call(s32[1]{0:T(128)} %bitcast.1.place_ref, bf16[8,144,2048]{2,1,0:T(8,128)(2,1)} %bitcast.90, f32[128,512]{1,0:T(8,128)} %get-tuple-element.53.query_ref, f32[128,512]{1,0:T(8,128)} %get-tuple-element.54.keys_ref, ...), custom_call_target="tpu_custom_call" | custom-call | tf_op jit(solution)/shard_map/forward_chain/pallas_call | solution.py:408
  218.6 1.6 multiply_reduce_fusion.4
  220.3 4.8 fusion.59
  225.1 1.9 fusion.4
  228.8 1.6 fusion.39.grad_ref
  230.4 6.2 backward_local.1
  236.6 11.2 %all-reduce.7.cloned.1.call-start = ((), (), s32[]{:S(2)}) async-start(), calls=%async_computation.8 | async-start | bytes 17301504
  247.9 3.6 fusion.31
  251.5 4.2 fusion.25
  255.7 23.8 %all-gather.13.cloned.1.call-done = bf16[4096,512]{1,0:T(8,128)(2,1)} async-done(((bf16[512,512]{1,0:T(8,128)(2,1)}), bf16[4096,512]{1,0:T(8,128)(2,1)}) %all-gather.13.cloned.1.call-update) | async-done | bytes 4194320 | tf_op jit(solution)/shard_map/all_gather | solution.py:544
  279.5 7.2 pad_maximum_fusion
  286.7 12.6 %reshape.210 = bf16[4,8,132,1024]{3,2,1,0:T(8,128)(2,1)} reshape(bf16[4224,1024]{1,0:T(8,128)(2,1)} %pad_maximum_fusion) | data formatting | bytes 17301504 | tf_op jit(solution)/shard_map/reshape | solution.py:434
  299.3 12.5 %copy.37 = bf16[4,8,132,1024]{3,0,2,1:T(4,128)(2,1)} copy(bf16[4,8,132,1024]{3,2,1,0:T(8,128)(2,1)} %reshape.210) | data formatting | bytes 17301504 | tf_op jit(solution)/shard_map/reshape | solution.py:434
  313.1 128.0 %all-reduce.7.cloned.1.call-done = bf16[4,8,132,1024]{3,0,2,1:T(4,128)(2,1)} async-done(((bf16[4,8,132,1024]{3,0,2,1:T(4,128)(2,1)}), bf16[4,8,132,1024]{3,0,2,1:T(4,128)(2,1)}) %all-reduce.7.cloned.1.call-update) | async-done | bytes 8650768
  441.1 2.3 dynamic-slice_bitcast_fusion
  444.8 23.2 %backward_chain.1 = (f32[128,2048]{1,0:T(8,128)}, f32[8,2048]{1,0:T(8,128)}, f32[8,2048]{1,0:T(8,128)}, f32[128,128]{1,0:T(8,128)}, f32[128,128]{1,0:T(8,128)}) custom-call(s32[1]{0:T(128)} %bitcast.1.place_ref, bf16[8,144,2048]{2,1,0:T(8,128)(2,1)} %bitcast.91, bf16[8,512,512]{2,1,0:T(8,128)(2,1)} %bitcast.95, f32[128,512]{1,0:T(8,128)} %get-tuple-element.53.query_ref, ...), custom_call_target="tpu_custom_call" | custom-call | tf_op jit(solution)/shard_map/backward_chain/pallas_call | solution.py:408
  467.9 1.5 collective-permute-start.1
  470.2 1.8 convert.18
  472.0 1.5 slice_add_fusion.1
  473.4 1.5 scatter-add.4
  477.0 5.5 fusion.23
  482.5 1.9 reshape.213
  484.4 7.0 pad_maximum_fusion.1
  492.3 3.1 fusion.1
  495.4 122.2 %all-reduce.9.cloned.1.call-done = bf16[4,8,128,1024]{3,2,1,0:T(8,128)(2,1)} async-done(((bf16[4,8,128,1024]{3,2,1,0:T(8,128)(2,1)}), bf16[4,8,128,1024]{3,2,1,0:T(8,128)(2,1)}) %all-reduce.9.cloned.1.call-update) | async-done | bytes 8388624
  617.6 3.0 dynamic-slice_bitcast_fusion.1
  621.8 3.8 fusion.24
  626.6 40.5 %psum.14 = f32[14852]{0:T(1024)S(1)} all-reduce(f32[14852]{0:T(1024)S(1)} %concatenate.21), channel_id=1, replica_groups=mesh['dp'=4,'ctx'=8] {'dp','ctx'}, use_global_device_ids=true, to_apply=%region_8.9 | all-reduce | flops 14852 | bytes 118816 | tf_op jit(solution)/shard_map/psum | solution.py:590
  672.5 40.2 %psum.15 = f32[]{:T(128)} all-reduce(f32[]{:T(128)S(6)} %add.148), channel_id=1, replica_groups=mesh['dp'=4,'ctx'=8] {'dp','ctx'}, use_global_device_ids=true, to_apply=%region_15.16 | all-reduce | flops 1 | bytes 8 | tf_op jit(solution)/shard_map/psum | solution.py:595
  714.8 2.7 multiply_subtract_fusion.1
  717.6 2.6 multiply_subtract_fusion
  (128 shorter events, 24.9 us)
Async XLA Ops:
  7.2 84.0 %all-gather.7.cloned.1.call-start = ((), (), s32[]{:S(2)}) async-start(), calls=%async_computation.2 | async-start | bytes 8650752 | tf_op jit(solution)/shard_map/all_gather | solution.py:469
  9.0 162.4 %all-gather.9.cloned.1.call-start = ((), (), s32[]{:S(2)}) async-start(), calls=%async_computation.3 | async-start | bytes 8921088 | tf_op jit(solution)/shard_map/all_gather | solution.py:470
  10.9 199.9 %all-gather.11.cloned.1.call-start = ((), (), s32[]{:S(2)}) async-start(), calls=%async_computation.6 | async-start | bytes 5308416 | tf_op jit(solution)/shard_map/all_gather | solution.py:497
  13.6 84.2 %copy-start.4 = (f32[1024,4]{1,0:T(8,128)}, f32[1024,4]{1,0:T(8,128)S(1)}, u32[]{:S(2)}) copy-start(f32[1024,4]{1,0:T(8,128)S(1)} %reshape.205) | copy-start | bytes 49156
  14.9 82.9 %copy-start.30 = (f32[128]{0:T(128)}, f32[128]{0:T(128)S(1)}, u32[]{:S(2)}) copy-start(f32[128]{0:T(128)S(1)} %fusion.15) | copy-start | bytes 1540
  15.7 82.0 %copy-start.25 = (f32[2]{0:T(128)}, f32[2]{0:T(128)S(1)}, u32[]{:S(2)}) copy-start(f32[2]{0:T(128)S(1)} %get-tuple-element.102) | copy-start | bytes 28
  15.7 82.1 %copy-start.27 = (f32[2]{0:T(128)}, f32[2]{0:T(128)S(1)}, u32[]{:S(2)}) copy-start(f32[2]{0:T(128)S(1)} %get-tuple-element.103) | copy-start | bytes 28
  97.8 10.4 %copy-start.1 = (bf16[1,128,1024]{2,1,0:T(8,128)(2,1)S(1)}, bf16[1,128,1024]{2,1,0:T(8,128)(2,1)}, u32[]{:S(2)}) copy-start(bf16[1,128,1024]{2,1,0:T(8,128)(2,1)} %param.13) | copy-start | bytes 786436
  108.2 18.2 %copy-start.19 = (f32[14852]{0:T(1024)S(1)}, f32[14852]{0:T(1024)}, u32[]{:S(2)}) copy-start(f32[14852]{0:T(1024)} %param.21) | copy-start | bytes 178228
  113.1 3.8 copy-start
  113.2 3.1 collective-permute-start
  126.3 153.2 %all-gather.13.cloned.1.call-start = ((), (), s32[]{:S(2)}) async-start(), calls=%async_computation.7 | async-start | bytes 4718592 | tf_op jit(solution)/shard_map/all_gather | solution.py:544
  218.6 6.5 copy-start.2
  218.6 6.5 copy-start.16
  220.3 6.7 slice-start
  225.1 2.3 slice-start.1
  227.0 1.6 copy-start.11
  227.0 3.4 copy-start.13
  230.4 21.1 %copy-start.12 = (bf16[128,1408]{1,0:T(8,128)(2,1)S(1)}, bf16[128,1408]{1,0:T(8,128)(2,1)}, u32[]{:S(2)}) copy-start(bf16[128,1408]{1,0:T(8,128)(2,1)} %copy-done.11) | copy-start | bytes 1081348
  230.4 21.1 %copy-start.14 = (bf16[128,1408]{1,0:T(8,128)(2,1)S(1)}, bf16[128,1408]{1,0:T(8,128)(2,1)}, u32[]{:S(2)}) copy-start(bf16[128,1408]{1,0:T(8,128)(2,1)} %copy-done.13) | copy-start | bytes 1081348
  236.6 204.4 %all-reduce.7.cloned.1.call-start = ((), (), s32[]{:S(2)}) async-start(), calls=%async_computation.8 | async-start | bytes 17301504
  311.8 0.7 copy-start.32
  311.9 170.6 %reduce-scatter.6.cloned.1.call-start = ((), (), s32[]{:S(2)}) async-start(), calls=%async_computation.4 | async-start | bytes 1392640 | tf_op jit(solution)/shard_map/reduce_scatter | solution.py:436
  444.7 172.9 %all-reduce.9.cloned.1.call-start = ((), (), s32[]{:S(2)}) async-start(), calls=%async_computation.9 | async-start | bytes 16777216
  444.7 24.7 %copy-start.17 = (bf16[128,1024]{1,0:T(8,128)(2,1)S(1)}, bf16[128,1024]{1,0:T(8,128)(2,1)}, u32[]{:S(2)}) copy-start(bf16[128,1024]{1,0:T(8,128)(2,1)} %get-tuple-element.57) | copy-start | bytes 786436
  467.9 4.0 collective-permute-start.1
  476.2 0.8 copy-start.7
  491.4 1.0 copy-start.15
  491.4 129.3 %copy-start.24 = (f32[8,2048]{1,0:T(8,128)S(1)}, f32[8,2048]{1,0:T(8,128)}, u32[]{:S(2)}) copy-start(f32[8,2048]{1,0:T(8,128)} %get-tuple-element.70) | copy-start | bytes 196612
  491.4 129.4 %copy-start.20 = (f32[128,128]{1,0:T(8,128)S(1)}, f32[128,128]{1,0:T(8,128)}, u32[]{:S(2)}) copy-start(f32[128,128]{1,0:T(8,128)} %get-tuple-element.68) | copy-start | bytes 196612
  491.4 129.4 %copy-start.21 = (f32[128,128]{1,0:T(8,128)S(1)}, f32[128,128]{1,0:T(8,128)}, u32[]{:S(2)}) copy-start(f32[128,128]{1,0:T(8,128)} %get-tuple-element.67) | copy-start | bytes 196612
  491.4 129.4 %copy-start.26 = (f32[2]{0:T(128)S(1)}, f32[2]{0:T(128)}, u32[]{:S(2)}) copy-start(f32[2]{0:T(128)} %copy-done.25) | copy-start | bytes 28
  491.4 129.4 %copy-start.28 = (f32[2]{0:T(128)S(1)}, f32[2]{0:T(128)}, u32[]{:S(2)}) copy-start(f32[2]{0:T(128)} %copy-done.27) | copy-start | bytes 28
  491.4 130.3 %copy-start.8 = (bf16[128,2048]{1,0:T(8,128)(2,1)S(1)}, bf16[128,2048]{1,0:T(8,128)(2,1)}, u32[]{:S(2)}) copy-start(bf16[128,2048]{1,0:T(8,128)(2,1)} %copy-done.7) | copy-start | bytes 1572868
  491.4 130.3 %copy-start.9 = (bf16[128,1024]{1,0:T(8,128)(2,1)S(1)}, bf16[128,1024]{1,0:T(8,128)(2,1)}, u32[]{:S(2)}) copy-start(bf16[128,1024]{1,0:T(8,128)(2,1)} %convert.18) | copy-start | bytes 786436
  491.4 177.3 %reduce-scatter.8.cloned.1.call-start = ((), (), s32[]{:S(2)}) async-start(), calls=%async_computation.5 | async-start | bytes 1310720 | tf_op jit(solution)/shard_map/reduce_scatter | solution.py:436
  620.6 5.0 copy-start.5
  620.7 5.8 copy-start.29
  620.8 46.4 %copy-start.31 = (f32[128]{0:T(128)S(1)}, f32[128]{0:T(128)}, u32[]{:S(2)}) copy-start(f32[128]{0:T(128)} %copy-done.30) | copy-start | bytes 1540
  621.7 46.3 %copy-start.3 = (f32[135168]{0:T(1024)S(1)}, f32[135168]{0:T(1024)}, u32[]{:S(2)}) copy-start(f32[135168]{0:T(1024)} %reshape.213) | copy-start | bytes 1622020
  621.8 92.3 %copy-start.22 = (f32[14852]{0:T(1024)S(1)}, f32[14852]{0:T(1024)}, u32[]{:S(2)}) copy-start(f32[14852]{0:T(1024)} %param.22) | copy-start | bytes 178228
  621.8 92.3 %copy-start.23 = (f32[14852]{0:T(1024)S(1)}, f32[14852]{0:T(1024)}, u32[]{:S(2)}) copy-start(f32[14852]{0:T(1024)} %param.23) | copy-start | bytes 178228
  625.6 91.9 %copy-start.10 = (f32[135168]{0:T(1024)S(1)}, f32[135168]{0:T(1024)}, u32[]{:S(2)}) copy-start(f32[135168]{0:T(1024)} %param.18) | copy-start | bytes 1622020
  667.1 53.1 %copy-start.18 = (f32[14852]{0:T(1024)}, f32[14852]{0:T(1024)S(1)}, u32[]{:S(2)}) copy-start(f32[14852]{0:T(1024)S(1)} %psum.14) | copy-start | bytes 178228
  669.9 50.3 %copy-start.6 = (f32[16,8,8,128]{3,1,2,0:T(8,128)}, f32[16,8,8,128]{3,1,2,0:T(8,128)S(1)}, u32[]{:S(2)}) copy-start(f32[16,8,8,128]{3,1,2,0:T(8,128)S(1)} %copy.44) | copy-start | bytes 1572868
Sparse Core Ops, SparseCore 0:
  11.4 79.7 all-gather.6
  94.7 76.6 all-gather.8
  173.3 37.4 all-gather.10
  236.8 42.7 all-gather.12
  312.0 129.0 all-reduce.6
  444.8 28.3 reduce-scatter.5
  491.5 126.0 all-reduce.8
  620.8 27.5 reduce-scatter.7
